TPU v7x, 256 devices: a whole 4x4x8 slice. The times are simulated.
256 devices in a mesh: expert: 16 (over y, x), hidden: 16 (over z, core).
Axes of the slice: x: 4, y: 4, z: 8, core: 2. Of those that a mesh axis runs over, the one named last changes fastest.
Arguments:
- layer_input: bfloat16 [4096, 4096], P('expert', 'hidden'), may hold values from -6 to 6
- output_grad: bfloat16 [4096, 4096], P('expert', 'hidden'), may hold values from -1.5 to 1.5
- latent_saved: bfloat16 [4096, 1024], P('expert'), may hold values from -6 to 6
- combined_saved: bfloat16 [4096, 1024], P('expert'), may hold values from -6 to 6
- expert_ids: int32 [4096, 22], P('expert'), may hold values from 0 to 511, as said below
- gate_values: bfloat16 [4096, 22], P('expert'), may hold values from 0.099609375 to 1.5
- down_proj: bfloat16 [1024, 4096], P(None, 'hidden'), may hold values from -0.09375 to 0.09375
- up_proj: bfloat16 [1024, 4096], P(None, 'hidden'), may hold values from -0.1875 to 0.1875
- expert_in: bfloat16 [16, 1024, 2688], P('expert', None, 'hidden'), may hold values from -0.1875 to 0.1875
- expert_out: bfloat16 [16, 2688, 1024], P('expert', 'hidden'), may hold values from -0.125 to 0.125
Outputs:
- input_grad: bfloat16 [4096, 4096], P('expert', 'hidden')
- down_grad: float32 [1024, 4096], P('expert', 'hidden')
- up_grad: float32 [1024, 4096], P('expert', 'hidden')
- gate_grad: float32 [4096, 22], P('expert')
- expert_in_grad: float32 [16, 1024, 2688], P('expert', None, 'hidden')
- expert_out_grad: float32 [16, 2688, 1024], P('expert', 'hidden')
Inputs may be any that keep to these rules, and one draw needn't show every extreme that they name: `expert_ids`: each row names 22 different experts. In each aligned block of 256 rows (the rows of one index of the expert axis) each expert below 16 is named by at most 24 rows; some expert below 16 is named by exactly 24 rows in every block.
All inputs are finite; a program needn't handle non-finite values.
Results may differ from a plain program's by a relative error of at most 0.0065.
Values may be sent and summed in bfloat16 or wider, within the bound.
No kernel may reach another device: no remote copies, remote signals or barrier semaphores. Data moves between devices by JAX's collectives and lax.ppermute only.
A program may use at most 64 MiB of HBM per device.

v0:
```python
import jax
import jax.numpy as jnp
from jax import lax
from jax.sharding import PartitionSpec as P


def slot_layout(table, groups, local_count):
    tokens_here = table.shape[0]
    return table.T.reshape(groups, local_count, tokens_here).transpose(1, 0, 2)[:, :, None, :]


def on_device(
    layer_input,
    output_grad,
    latent_saved,
    combined_saved,
    expert_ids,
    gate_values,
    down_proj,
    up_proj,
    expert_in,
    expert_out,
):
    groups = lax.axis_size("expert")
    tokens_here = layer_input.shape[0]
    latent_width = latent_saved.shape[1]
    local_count = expert_in.shape[0]
    capacity = tokens_here * 3 // 32
    live_count = local_count * groups
    slot_total = local_count * groups * capacity
    partial_cot = jnp.einsum("td,ld->tl", output_grad, up_proj, preferred_element_type=jnp.float32)
    member = expert_ids[:, :, None] == jnp.arange(live_count, dtype=jnp.int32)[None, None, :]
    per_token = jnp.sum(member.astype(jnp.int32), axis=1)
    before = jnp.cumsum(per_token, axis=0) - per_token
    gate_token = jnp.sum(
        jnp.where(member, gate_values.astype(jnp.float32)[:, :, None], 0.0), axis=1
    )
    rank_iota = jnp.arange(capacity, dtype=jnp.int32)[None, None, :, None]
    hit_slot = (slot_layout(per_token, groups, local_count) == 1) & (
        slot_layout(before, groups, local_count) == rank_iota
    )
    gate_slot = jnp.sum(
        jnp.where(hit_slot, slot_layout(gate_token, groups, local_count), 0.0), axis=3
    )
    gate_send = gate_slot.astype(jnp.bfloat16)
    dispatch_bf = hit_slot.astype(jnp.bfloat16).reshape(slot_total, tokens_here)
    cot_full = lax.psum(partial_cot, "hidden")
    cot_rows = jnp.dot(
        dispatch_bf, cot_full.astype(jnp.bfloat16), preferred_element_type=jnp.float32
    ).astype(jnp.bfloat16)
    latent_rows = jnp.dot(dispatch_bf, latent_saved, preferred_element_type=jnp.float32).astype(
        jnp.bfloat16
    )
    cot_recv, latent_recv, gate_recv = (
        lax.all_to_all(
            cot_rows.reshape(local_count, groups, capacity, latent_width),
            "expert",
            split_axis=1,
            concat_axis=1,
            tiled=True,
        ),
        lax.all_to_all(
            latent_rows.reshape(local_count, groups, capacity, latent_width),
            "expert",
            split_axis=1,
            concat_axis=1,
            tiled=True,
        ),
        lax.all_to_all(gate_send, "expert", split_axis=1, concat_axis=1, tiled=True),
    )
    row_count = groups * capacity
    cot_block = cot_recv.reshape(local_count, row_count, latent_width)
    latent_block = latent_recv.reshape(local_count, row_count, latent_width)
    gate_block = gate_recv.reshape(local_count, row_count).astype(jnp.float32)
    pre_act = jnp.einsum(
        "erl,elf->erf", latent_block, expert_in, preferred_element_type=jnp.float32
    )
    relu_out = jnp.maximum(pre_act, 0.0)
    back_proj = jnp.einsum(
        "erl,efl->erf", cot_block, expert_out, preferred_element_type=jnp.float32
    )
    gate_part = jnp.sum(back_proj * relu_out * relu_out, axis=2)
    scaled_act = (gate_block[:, :, None] * relu_out * relu_out).astype(jnp.bfloat16)
    pre_grad = (2.0 * gate_block[:, :, None] * relu_out * back_proj).astype(jnp.bfloat16)
    expert_out_grad = jnp.einsum(
        "erf,erl->efl", scaled_act, cot_block, preferred_element_type=jnp.float32
    )
    expert_in_grad = jnp.einsum(
        "erl,erf->elf", latent_block, pre_grad, preferred_element_type=jnp.float32
    )
    latent_back = jnp.einsum(
        "erf,elf->erl", pre_grad, expert_in, preferred_element_type=jnp.float32
    )
    latent_back = latent_back.reshape(local_count, groups, capacity, latent_width)
    gate_part = gate_part.reshape(local_count, groups, capacity)
    dispatch_full = hit_slot.astype(jnp.float32)
    dispatch_flat = dispatch_full.reshape(slot_total, tokens_here)
    rows_home, gate_home = (
        lax.all_to_all(latent_back, "expert", split_axis=1, concat_axis=1, tiled=True),
        lax.all_to_all(gate_part, "expert", split_axis=1, concat_axis=1, tiled=True),
    )
    token_sums = jnp.dot(
        dispatch_flat.T,
        rows_home.reshape(slot_total, latent_width),
        precision=lax.Precision.HIGHEST,
        preferred_element_type=jnp.float32,
    )
    by_expert = jnp.sum(dispatch_full * gate_home[:, :, :, None], axis=2)
    by_expert = by_expert.transpose(2, 1, 0).reshape(tokens_here, live_count)
    gate_local = jnp.sum(jnp.where(member, by_expert[:, None, :], 0.0), axis=2)
    latent_grad, gate_grad = lax.psum((token_sums, gate_local), "hidden")
    latent_bf = latent_grad.astype(jnp.bfloat16)
    input_grad = jnp.dot(latent_bf, down_proj, preferred_element_type=jnp.float32).astype(
        jnp.bfloat16
    )
    down_term = jnp.einsum("tl,td->ld", latent_bf, layer_input, preferred_element_type=jnp.float32)
    up_term = jnp.einsum(
        "tl,td->ld", combined_saved, output_grad, preferred_element_type=jnp.float32
    )
    down_grad, up_grad = (
        lax.psum_scatter(down_term, "expert", scatter_dimension=0, tiled=True),
        lax.psum_scatter(up_term, "expert", scatter_dimension=0, tiled=True),
    )
    return (input_grad, down_grad, up_grad, gate_grad, expert_in_grad, expert_out_grad)


def solution(mesh):
    return jax.shard_map(
        on_device,
        mesh=mesh,
        in_specs=(
            P("expert", "hidden"),
            P("expert", "hidden"),
            P("expert", None),
            P("expert", None),
            P("expert", None),
            P("expert", None),
            P(None, "hidden"),
            P(None, "hidden"),
            P("expert", None, "hidden"),
            P("expert", "hidden", None),
        ),
        out_specs=(
            P("expert", "hidden"),
            P("expert", "hidden"),
            P("expert", "hidden"),
            P("expert", None),
            P("expert", None, "hidden"),
            P("expert", "hidden", None),
        ),
        check_vma=False,
    )
```

profile of v0, /device:TPU:2, one launch (start us, length us, event | category | flops | bytes accessed | tf_op | source)
XLA Modules:
  0.0 312.9 jit_solution(7600036610667485425)
XLA Ops:
  7.2 0.8 convert_reduce_fusion
  9.0 1.5 fusion.23
  10.5 62.0 %all-reduce.3 = bf16[256,1024]{1,0:T(8,128)(2,1)S(1)} all-reduce(f32[256,1024]{1,0:T(8,128)S(1)} %fusion.23), channel_id=1, replica_groups=mesh['expert'=16,'hidden'=16] {'hidden'}, use_global_device_ids=true, to_apply=%region_5.6 | all-reduce | flops 262144 | bytes 1572864 | tf_op jit(solution)/shard_map/psum | solution.py:47
  72.7 1.3 convolution_convert_fusion
  73.9 7.5 %all-to-all-start.2 = ((bf16[1,16,24,1024]{3,2,0,1:T(8,128)(2,1)}), bf16[1,16,24,1024]{3,2,0,1:T(8,128)(2,1)S(1)}, u32[]{:S(2)}, u32[]{:S(2)}) async-start(bf16[1,16,24,1024]{3,2,0,1:T(8,128)(2,1)} %bitcast.11), calls=%async_computation.2 | async-start | bytes 1572864 | tf_op jit(solution)/shard_map/all_to_all | solution.py:55
  81.4 1.3 convolution_convert_fusion.1
  82.7 8.9 %all-to-all-done.2 = bf16[1,16,24,1024]{3,2,0,1:T(8,128)(2,1)S(1)} async-done(((bf16[1,16,24,1024]{3,2,0,1:T(8,128)(2,1)}), bf16[1,16,24,1024]{3,2,0,1:T(8,128)(2,1)S(1)}, u32[]{:S(2)}, u32[]{:S(2)}) %all-to-all-start.2) | async-done | bytes 786464 | tf_op jit(solution)/shard_map/all_to_all | solution.py:55
  91.6 4.9 %all-to-all-start.1 = ((bf16[1,16,24,1024]{3,2,0,1:T(8,128)(2,1)}), bf16[1,16,24,1024]{3,2,0,1:T(8,128)(2,1)S(1)}, u32[]{:S(2)}, u32[]{:S(2)}) async-start(bf16[1,16,24,1024]{3,2,0,1:T(8,128)(2,1)} %bitcast.7), calls=%async_computation.1 | async-start | bytes 1572864 | tf_op jit(solution)/shard_map/all_to_all | solution.py:62
  96.9 9.9 %all-to-all-done.1 = bf16[1,16,24,1024]{3,2,0,1:T(8,128)(2,1)S(1)} async-done(((bf16[1,16,24,1024]{3,2,0,1:T(8,128)(2,1)}), bf16[1,16,24,1024]{3,2,0,1:T(8,128)(2,1)S(1)}, u32[]{:S(2)}, u32[]{:S(2)}) %all-to-all-start.1) | async-done | bytes 786464 | tf_op jit(solution)/shard_map/all_to_all | solution.py:62
  107.2 0.7 reshape.184
  107.9 4.7 %all-to-all-start.4 = ((f32[1,16,24]{2,0,1:T(1,128)}), f32[1,16,24]{2,0,1:T(1,128)S(1)}, u32[]{:S(2)}, u32[]{:S(2)}) async-start(f32[1,16,24]{2,0,1:T(1,128)} %reshape.184), calls=%async_computation.6 | async-start | bytes 16384 | tf_op jit(solution)/shard_map/all_to_all | solution.py:100
  112.7 6.2 %all-to-all-done.4 = f32[1,16,24]{2,0,1:T(1,128)S(1)} async-done(((f32[1,16,24]{2,0,1:T(1,128)}), f32[1,16,24]{2,0,1:T(1,128)S(1)}, u32[]{:S(2)}, u32[]{:S(2)}) %all-to-all-start.4) | async-done | bytes 1568 | tf_op jit(solution)/shard_map/all_to_all | solution.py:100
  119.4 10.6 %all_to_all.25 = bf16[1,16,24]{2,0,1:T(2,128)(2,1)S(1)} all-to-all(bf16[1,16,24]{2,0,1:T(2,128)(2,1)S(1)} %copy.45), channel_id=1, replica_groups=mesh['expert'=16,'hidden'=16] {'expert'}, dimensions={1} | all-to-all | bytes 1536 | tf_op jit(solution)/shard_map/all_to_all | solution.py:69
  130.3 1.5 convolution_bitcast_fusion
  131.8 5.7 %all-to-all-start.3 = ((f32[1,16,24,1024]{3,2,0,1:T(8,128)}), f32[1,16,24,1024]{3,2,0,1:T(8,128)}, u32[]{:S(2)}, u32[]{:S(2)}) async-start(f32[1,16,24,1024]{3,2,0,1:T(8,128)} %convolution_bitcast_fusion), calls=%async_computation.3 | async-start | bytes 3145728 | tf_op jit(solution)/shard_map/all_to_all | solution.py:99
  137.6 1.3 fusion.24
  139.0 13.1 %all-to-all-done.3 = f32[1,16,24,1024]{3,2,0,1:T(8,128)} async-done(((f32[1,16,24,1024]{3,2,0,1:T(8,128)}), f32[1,16,24,1024]{3,2,0,1:T(8,128)}, u32[]{:S(2)}, u32[]{:S(2)}) %all-to-all-start.3) | async-done | bytes 1572896 | tf_op jit(solution)/shard_map/all_to_all | solution.py:99
  152.1 3.5 %fusion.2 = f32[256,1024]{1,0:T(8,128)} fusion(f32[1,16,24,1024]{3,2,0,1:T(8,128)} %all-to-all-done.3, s32[16,256]{1,0:T(8,128)S(1)} %bitcast_subtract_fusion, pred[16,256]{1,0:T(8,128)(4,1)S(1)} %bitcast_compare_fusion.1), kind=kOutput, calls=%fused_computation.5 | convolution fusion | flops 1208156160 | bytes 2641920 | tf_op jit(solution)/shard_map/dot_general | solution.py:102
  155.7 66.5 %all-reduce.4 = (bf16[256,1024]{1,0:T(8,128)(2,1)S(1)}, f32[256,22]{0,1:T(8,128)}) all-reduce(f32[256,1024]{1,0:T(8,128)} %fusion.2, f32[256,22]{0,1:T(8,128)S(1)} %get-tuple-element.6), channel_id=1, replica_groups=mesh['expert'=16,'hidden'=16] {'hidden'}, use_global_device_ids=true, to_apply=%region_6.7 | all-reduce | flops 267776 | bytes 1617920 | tf_op jit(solution)/shard_map/psum | solution.py:111
  222.1 1.3 fusion.25
  223.5 1.2 convolution_bitcast_fusion.2
  224.7 1.2 convolution_bitcast_fusion.1
  225.9 1.0 convolution_convert_fusion.2
  226.9 79.2 %reduce-scatter.3.cloned.1.call-done = f32[64,256]{1,0:T(8,128)} async-done(((f32[1024,256]{1,0:T(8,128)}), f32[64,256]{1,0:T(8,128)}) %reduce-scatter.3.cloned.1.call-update) | async-done | bytes 65552 | tf_op jit(solution)/shard_map/reduce_scatter | solution.py:121
  (45 shorter events, 2.9 us)
Async XLA Ops:
  7.2 74.3 %copy-start = (bf16[256,1024]{1,0:T(8,128)(2,1)S(1)}, bf16[256,1024]{1,0:T(8,128)(2,1)}, u32[]{:S(2)}) copy-start(bf16[256,1024]{1,0:T(8,128)(2,1)} %param.12) | copy-start | bytes 1572868
  73.9 17.7 %all-to-all-start.2 = ((bf16[1,16,24,1024]{3,2,0,1:T(8,128)(2,1)}), bf16[1,16,24,1024]{3,2,0,1:T(8,128)(2,1)S(1)}, u32[]{:S(2)}, u32[]{:S(2)}) async-start(bf16[1,16,24,1024]{3,2,0,1:T(8,128)(2,1)} %bitcast.11), calls=%async_computation.2 | async-start | bytes 1572864 | tf_op jit(solution)/shard_map/all_to_all | solution.py:55
  81.4 15.1 %copy-start.5 = (bf16[1,168,1024]{2,1,0:T(8,128)(2,1)S(1)}, bf16[1,168,1024]{2,1,0:T(8,128)(2,1)}, u32[]{:S(2)}) copy-start(bf16[1,168,1024]{2,1,0:T(8,128)(2,1)} %param.19) | copy-start | bytes 1032196
  82.7 24.0 %copy-start.1 = (bf16[1,1024,168]{1,2,0:T(8,128)(2,1)S(1)}, bf16[1,1024,168]{1,2,0:T(8,128)(2,1)}, u32[]{:S(2)}) copy-start(bf16[1,1024,168]{1,2,0:T(8,128)(2,1)} %param.18) | copy-start | bytes 1032196
  91.6 15.2 %all-to-all-start.1 = ((bf16[1,16,24,1024]{3,2,0,1:T(8,128)(2,1)}), bf16[1,16,24,1024]{3,2,0,1:T(8,128)(2,1)S(1)}, u32[]{:S(2)}, u32[]{:S(2)}) async-start(bf16[1,16,24,1024]{3,2,0,1:T(8,128)(2,1)} %bitcast.7), calls=%async_computation.1 | async-start | bytes 1572864 | tf_op jit(solution)/shard_map/all_to_all | solution.py:62
  96.5 16.2 %copy-start.8 = (bf16[256,22]{0,1:T(8,128)(2,1)S(1)}, bf16[256,22]{0,1:T(8,128)(2,1)}, u32[]{:S(2)}) copy-start(bf16[256,22]{0,1:T(8,128)(2,1)} %param.15) | copy-start | bytes 33796
  96.5 22.5 %copy-start.7 = (s32[256,22]{0,1:T(8,128)S(1)}, s32[256,22]{0,1:T(8,128)}, u32[]{:S(2)}) copy-start(s32[256,22]{0,1:T(8,128)} %param.14) | copy-start | bytes 67588
  107.9 10.9 %all-to-all-start.4 = ((f32[1,16,24]{2,0,1:T(1,128)}), f32[1,16,24]{2,0,1:T(1,128)S(1)}, u32[]{:S(2)}, u32[]{:S(2)}) async-start(f32[1,16,24]{2,0,1:T(1,128)} %reshape.184), calls=%async_computation.6 | async-start | bytes 16384 | tf_op jit(solution)/shard_map/all_to_all | solution.py:100
  131.8 5.8 %copy-start.2 = (bf16[256,1024]{1,0:T(8,128)(2,1)S(1)}, bf16[256,1024]{1,0:T(8,128)(2,1)}, u32[]{:S(2)}) copy-start(bf16[256,1024]{1,0:T(8,128)(2,1)} %param.13) | copy-start | bytes 1572868
  131.8 5.8 %copy-start.4 = (bf16[256,256]{1,0:T(8,128)(2,1)S(1)}, bf16[256,256]{1,0:T(8,128)(2,1)}, u32[]{:S(2)}) copy-start(bf16[256,256]{1,0:T(8,128)(2,1)} %param.11) | copy-start | bytes 393220
  131.8 20.3 %all-to-all-start.3 = ((f32[1,16,24,1024]{3,2,0,1:T(8,128)}), f32[1,16,24,1024]{3,2,0,1:T(8,128)}, u32[]{:S(2)}, u32[]{:S(2)}) async-start(f32[1,16,24,1024]{3,2,0,1:T(8,128)} %convolution_bitcast_fusion), calls=%async_computation.3 | async-start | bytes 3145728 | tf_op jit(solution)/shard_map/all_to_all | solution.py:99
  137.5 89.4 %reduce-scatter.5.cloned.1.call-start = ((), (), s32[]{:S(2)}) async-start(), calls=%async_computation.8 | async-start | bytes 1114112 | tf_op jit(solution)/shard_map/reduce_scatter | solution.py:122
  138.9 83.2 %copy-start.6 = (bf16[256,256]{1,0:T(8,128)(2,1)S(1)}, bf16[256,256]{1,0:T(8,128)(2,1)}, u32[]{:S(2)}) copy-start(bf16[256,256]{1,0:T(8,128)(2,1)} %param.10) | copy-start | bytes 393220
  138.9 167.1 %reduce-scatter.3.cloned.1.call-start = ((), (), s32[]{:S(2)}) async-start(), calls=%async_computation.7 | async-start | bytes 1114112 | tf_op jit(solution)/shard_map/reduce_scatter | solution.py:121
  223.5 2.4 copy-start.3
Sparse Core Ops, SparseCore 0:
  142.4 81.0 reduce-scatter.4
  227.6 78.4 reduce-scatter.2
where the time goes:
time: 313 us
  blocking collectives  139 us (44%)
  waiting for transfers between devices  117 us (37%)
  starting transfers between devices  22.9 us (7%)
  matrix products  15.9 us (5%)
  between operations  14.3 us (5%)
    reduce_scatter x1, waiting for transfers between devices, on_device(): lax.psum_scatter(down_term, 'expert', scatter_dimension=0, tiled=True)  79.2 us
    psum x1, blocking collectives, on_device(): latent_grad, gate_grad = lax.psum((token_sums, gate_local), 'hidden')  66.5 us
    psum x1, blocking collectives, on_device(): cot_full = lax.psum(partial_cot, 'hidden')  62 us
    all_to_all x1, waiting for transfers between devices, on_device(): lax.all_to_all(latent_back, 'expert', split_axis=1, concat_axis=1, tiled=...  13.1 us
    all_to_all x1, blocking collectives, on_device(): lax.all_to_all(gate_send, 'expert', split_axis=1, concat_axis=1, tiled=True)  10.6 us
    all_to_all x1, waiting for transfers between devices, on_device(): lax.all_to_all(latent_rows.reshape(local_count, groups, capacity, latent_...  9.86 us
    all_to_all x1, waiting for transfers between devices, on_device(): lax.all_to_all(cot_rows.reshape(local_count, groups, capacity, latent_wid...  8.87 us
    all_to_all x1, starting transfers between devices, on_device(): lax.all_to_all(cot_rows.reshape(local_count, groups, capacity, latent_wid...  7.48 us
  transfers between devices with their start and end apart: 6, of which 5 were waited for; matrix products, arithmetic and copies ran while one was open for 4% of the time, Pallas kernels for 0%

commit v1 on v0

v1 whole, which is shorter than its diff:
```python
import jax
import jax.numpy as jnp
from jax import lax
from jax.sharding import PartitionSpec as P

BF = jnp.bfloat16
F32 = jnp.float32


def mm(a, b, dims):
    return lax.dot_general(a, b, (dims, ((), ())), preferred_element_type=F32)


def on_device(
    layer_input,
    output_grad,
    latent_saved,
    combined_saved,
    expert_ids,
    gate_values,
    down_proj,
    up_proj,
    expert_in,
    expert_out,
):
    groups = lax.axis_size("expert")
    width = lax.axis_size("hidden")
    half = width // 2
    tokens_here = layer_input.shape[0]
    latent_width = latent_saved.shape[1]
    capacity = tokens_here * 3 // 32
    lanes = 128
    shard = lax.axis_index("expert")
    slot = lax.axis_index("hidden")
    ring, core = slot // 2, slot % 2

    pair_perm = [(i, i ^ 1) for i in range(width)]
    ring_groups = [[2 * i + c for i in range(half)] for c in range(2)]
    move_perm = [
        (t * width + j, (t ^ j) * width + j) for t in range(groups) for j in range(width)
    ]

    def pair_swap(x):
        m = x.shape[0] // 2
        return jnp.concatenate(
            [lax.ppermute(x[:m], "hidden", pair_perm), lax.ppermute(x[m:], "hidden", pair_perm)]
        )

    def ring_exchange(x):
        return lax.all_to_all(x, "hidden", 0, 0, tiled=True, axis_index_groups=ring_groups)

    def ring_gather(x):
        return ring_exchange(jnp.broadcast_to(x[None], (half,) + x.shape))

    def move(x):
        return lax.ppermute(x, ("expert", "hidden"), move_perm)

    steps = 2 * jnp.arange(half, dtype=jnp.int32)
    experts = shard ^ jnp.concatenate([steps + core, steps + 1 - core])
    ids_t = expert_ids.T
    member = ids_t[None] == experts[:, None, None]
    routed = jnp.any(member, axis=1)
    tri = (
        lax.broadcasted_iota(jnp.int32, (tokens_here, tokens_here), 0)
        < lax.broadcasted_iota(jnp.int32, (tokens_here, tokens_here), 1)
    ).astype(BF)
    before = mm(routed.astype(BF), tri, ((1,), (0,)))
    rank = lax.broadcasted_iota(jnp.int32, (1, capacity, 1), 1).astype(F32)
    hit = routed[:, None, :] & (before[:, None, :] == rank)
    picks = hit.astype(BF)
    rows = half * capacity
    pick_own = picks[:half].reshape(rows, tokens_here)
    pick_oth = picks[half:].reshape(rows, tokens_here)
    pick_here = lax.dynamic_index_in_dim(picks[:half], ring, 0, False)

    gate_token = jnp.sum(
        jnp.where(ids_t == (shard ^ slot), gate_values.T.astype(F32), 0.0), axis=0
    ).astype(BF)
    gate_cols = jnp.broadcast_to(gate_token[:, None], (tokens_here, lanes))
    latent_block = jnp.concatenate(
        [mm(pick_here, latent_saved, ((1,), (0,))), mm(pick_here, gate_cols, ((1,), (0,)))], axis=1
    ).astype(BF)
    latent_own = ring_gather(move(latent_block)).reshape(rows, latent_width + lanes)
    latent_oth = pair_swap(latent_own)

    def cot_part(pick):
        grads = mm(pick, output_grad, ((1,), (0,))).astype(BF)
        return mm(grads, up_proj, ((1,), (1,)))

    cot_sum = cot_part(pick_own) + pair_swap(cot_part(pick_oth).astype(BF)).astype(F32)
    cot_got = ring_exchange(cot_sum.astype(BF).reshape(half, capacity, latent_width))
    cot_block = jnp.sum(cot_got.astype(F32), axis=0).astype(BF)
    cot_own = ring_gather(move(cot_block)).reshape(rows, latent_width)
    cot_oth = pair_swap(cot_own)

    w_in = expert_in[0]
    w_out = expert_out[0]
    latent_all = jnp.concatenate([latent_own, latent_oth])
    cot_all = jnp.concatenate([cot_own, cot_oth])
    latent_rows = latent_all[:, :latent_width]
    gate_rows = latent_all[:, latent_width : latent_width + 1].astype(F32)
    act = jnp.maximum(mm(latent_rows, w_in, ((1,), (0,))), 0.0)
    back = mm(cot_all, w_out, ((1,), (1,)))
    gate_part = jnp.sum(back * act * act, axis=1, keepdims=True)
    scaled = (gate_rows * act * act).astype(BF)
    pre_grad = (2.0 * gate_rows * act * back).astype(BF)
    latent_back = mm(pre_grad, w_in, ((1,), (1,)))

    lane = lax.broadcasted_iota(jnp.int32, (1, lanes), 1)

    def pack(main, gate, hi_lane, lo_lane):
        hi = gate.astype(BF)
        lo = (gate - hi.astype(F32)).astype(BF)
        side = jnp.where(lane == hi_lane, hi, jnp.where(lane == lo_lane, lo, jnp.zeros((), BF)))
        return jnp.concatenate([main.astype(BF), side], axis=-1)

    def unpack(x):
        x = x.astype(F32)
        gate = x[..., latent_width : latent_width + 1] + x[..., latent_width + 1 : latent_width + 2]
        return x[..., :latent_width], gate

    got_main, got_gate = unpack(pair_swap(pack(latent_back[rows:], gate_part[rows:], 0, 1)))
    main = latent_back[:rows] + got_main
    gate = gate_part[:rows] + got_gate
    back_got = ring_exchange(pack(main, gate, 0, 1).reshape(half, capacity, latent_width + lanes))
    main, gate = unpack(jnp.sum(back_got.astype(F32), axis=0))
    home = move(pack(main, gate, slot, width + slot))
    home_own = ring_gather(home).reshape(rows, latent_width + lanes)
    home_oth = pair_swap(home_own)
    sums = mm(pick_own, home_own, ((0,), (0,))) + mm(pick_oth, home_oth, ((0,), (0,)))
    latent_bf = sums[:, :latent_width].astype(BF)
    by_block = (
        sums[:, latent_width : latent_width + width]
        + sums[:, latent_width + width : latent_width + 2 * width]
    )
    blocks = shard ^ jnp.arange(width, dtype=jnp.int32)
    gate_grad = jnp.sum(
        jnp.where(expert_ids[:, :, None] == blocks, by_block[:, None, :], 0.0), axis=2
    )

    input_grad = mm(latent_bf, down_proj, ((1,), (0,))).astype(BF)
    share = latent_width // groups

    def spread(a, b):
        part = mm(a, b, ((0,), (0,))).astype(BF).reshape(groups, share, b.shape[1])
        got = lax.all_to_all(part, "expert", 0, 0, tiled=True)
        return jnp.sum(got.astype(F32), axis=0)

    up_grad = spread(combined_saved, output_grad)
    down_grad = spread(latent_bf, layer_input)
    expert_out_grad = mm(scaled, cot_all, ((0,), (0,)))[None]
    expert_in_grad = mm(latent_rows, pre_grad, ((0,), (0,)))[None]
    return (input_grad, down_grad, up_grad, gate_grad, expert_in_grad, expert_out_grad)


def solution(mesh):
    return jax.shard_map(
        on_device,
        mesh=mesh,
        in_specs=(
            P("expert", "hidden"),
            P("expert", "hidden"),
            P("expert", None),
            P("expert", None),
            P("expert", None),
            P("expert", None),
            P(None, "hidden"),
            P(None, "hidden"),
            P("expert", None, "hidden"),
            P("expert", "hidden", None),
        ),
        out_specs=(
            P("expert", "hidden"),
            P("expert", "hidden"),
            P("expert", "hidden"),
            P("expert", None),
            P("expert", None, "hidden"),
            P("expert", "hidden", None),
        ),
        check_vma=False,
    )
```

time: 313 us -> 158 us (0.50)
  blocking collectives: 139 us -> 0 us
  waiting for transfers between devices: 117 us -> 93.6 us
  starting transfers between devices: 22.9 us -> 40.6 us
  between operations: 14.3 us -> 1.16 us
  matrix products: 15.9 us -> 11 us
  other arithmetic: 2.22 us -> 5.55 us
    psum x2 -> x0, blocking collectives: 128 us -> none  [the longest x1 66.5 us: on_device(): latent_grad, gate_grad = lax.psum((token_sums, gate_local), 'hidden')]
    reduce_scatter x2 -> x0, waiting for transfers between devices: 79.2 us -> none  [the longest x1 79.2 us: on_device(): lax.psum_scatter(down_term, 'expert', scatter_dimension=0, tiled=True)]
    all_to_all x4 -> x7, waiting for transfers between devices: 38.1 us -> 88.9 us  [the longest x5 70.4 us: ring_exchange(): lax.all_to_all(x, 'hidden', 0, 0, tiled=True, axis_index_groups=ring_groups)]
    all_to_all x4 -> x7, starting transfers between devices: 22.8 us -> 35.6 us  [the longest x5 22.5 us: ring_exchange(): lax.all_to_all(x, 'hidden', 0, 0, tiled=True, axis_index_groups=ring_groups)]
    all_to_all x1 -> x0, blocking collectives: 10.6 us -> none  [on_device(): lax.all_to_all(gate_send, 'expert', split_axis=1, concat_axis=1, tiled=True)]
    ppermute x0 -> x13, starting transfers between devices: none -> 4.96 us  [the longest x3 1.99 us: move(): return lax.ppermute(x, ('expert', 'hidden'), move_perm)]
    dot_general x12 -> x15, matrix products: 15.9 us -> 11 us  [mm(): return lax.dot_general(a, b, (dims, ((), ())), preferred_element_type=F32)]
    ppermute x0 -> x13, waiting for transfers between devices: none -> 4.74 us  [the longest x5 2.57 us: pair_swap(): lax.ppermute(x[:m], 'hidden', pair_perm)]
  transfers between devices with their start and end apart: 6 -> 20, of which waited for: 5 -> 15; matrix products, arithmetic and copies ran while one was open for 4% -> 5% of each run, Pallas kernels for 0% -> 0%
where the time goes in v1:
time: 158 us; the launch traced here: 156 us
  waiting for transfers between devices  93.6 us (59%)
  starting transfers between devices  40.6 us (26%)
  matrix products  11 us (7%)
  other arithmetic  5.55 us (4%)
  local copies, waits for them, and re-layouts  4.32 us (3%)
    all_to_all x5, waiting for transfers between devices, ring_exchange(): lax.all_to_all(x, 'hidden', 0, 0, tiled=True, axis_index_groups=ring_groups)  70.4 us
    all_to_all x5, starting transfers between devices, ring_exchange(): lax.all_to_all(x, 'hidden', 0, 0, tiled=True, axis_index_groups=ring_groups)  22.5 us
    all_to_all x2, waiting for transfers between devices, spread(): got = lax.all_to_all(part, 'expert', 0, 0, tiled=True)  18.5 us
    all_to_all x2, starting transfers between devices, spread(): got = lax.all_to_all(part, 'expert', 0, 0, tiled=True)  13.2 us
    dot_general x15, matrix products, mm(): return lax.dot_general(a, b, (dims, ((), ())), preferred_element_type=F32)  11 us
  transfers between devices with their start and end apart: 20, of which 15 were waited for; matrix products, arithmetic and copies ran while one was open for 5% of the time, Pallas kernels for 0%

profile of v1, /device:TPU:2, one launch (start us, length us, event | category | flops | bytes accessed | tf_op | source)
XLA Modules:
  0.0 156.2 jit_solution(16647814157202583779)
XLA Ops:
  2.1 1.3 convolution_convert_fusion.2
  5.3 1.2 add_convert_fusion
  6.5 8.5 %all-to-all-start.1 = ((bf16[8,24,1024]{2,1,0:T(8,128)(2,1)}), bf16[8,24,1024]{2,1,0:T(8,128)(2,1)S(1)}, u32[]{:S(2)}, u32[]{:S(2)}) async-start(bf16[8,24,1024]{2,1,0:T(8,128)(2,1)} %bitcast.9), calls=%async_computation.1 | async-start | bytes 786432 | tf_op jit(solution)/shard_map/all_to_all | solution.py:50
  16.0 14.0 %all-to-all-done.1 = bf16[8,24,1024]{2,1,0:T(8,128)(2,1)S(1)} async-done(((bf16[8,24,1024]{2,1,0:T(8,128)(2,1)}), bf16[8,24,1024]{2,1,0:T(8,128)(2,1)S(1)}, u32[]{:S(2)}, u32[]{:S(2)}) %all-to-all-start.1) | async-done | bytes 393248 | tf_op jit(solution)/shard_map/all_to_all | solution.py:50
  30.8 3.5 %all-to-all-start = ((bf16[8,24,1152]{2,1,0:T(8,128)(2,1)}), bf16[8,24,1152]{2,1,0:T(8,128)(2,1)S(1)}, u32[]{:S(2)}, u32[]{:S(2)}) async-start(bf16[8,24,1152]{2,1,0:T(8,128)(2,1)} %broadcast_in_dim.157), calls=%async_computation | async-start | bytes 884736 | tf_op jit(solution)/shard_map/all_to_all | solution.py:50
  35.0 15.4 %all-to-all-done = bf16[8,24,1152]{2,1,0:T(8,128)(2,1)S(1)} async-done(((bf16[8,24,1152]{2,1,0:T(8,128)(2,1)}), bf16[8,24,1152]{2,1,0:T(8,128)(2,1)S(1)}, u32[]{:S(2)}, u32[]{:S(2)}) %all-to-all-start) | async-done | bytes 442400 | tf_op jit(solution)/shard_map/all_to_all | solution.py:50
  51.2 3.6 %all-to-all-start.2 = ((bf16[8,24,1024]{2,1,0:T(8,128)(2,1)}), bf16[8,24,1024]{2,1,0:T(8,128)(2,1)S(1)}, u32[]{:S(2)}, u32[]{:S(2)}) async-start(bf16[8,24,1024]{2,1,0:T(8,128)(2,1)} %broadcast_in_dim.158), calls=%async_computation.2 | async-start | bytes 786432 | tf_op jit(solution)/shard_map/all_to_all | solution.py:50
  55.4 1.0 collective-permute-done.2
  57.4 12.5 %all-to-all-done.2 = bf16[8,24,1024]{2,1,0:T(8,128)(2,1)S(1)} async-done(((bf16[8,24,1024]{2,1,0:T(8,128)(2,1)}), bf16[8,24,1024]{2,1,0:T(8,128)(2,1)S(1)}, u32[]{:S(2)}, u32[]{:S(2)}) %all-to-all-start.2) | async-done | bytes 393248 | tf_op jit(solution)/shard_map/all_to_all | solution.py:50
  73.9 1.1 collective-permute-done.8
  76.1 1.0 copy.37
  77.1 3.5 %all-to-all-start.3 = ((bf16[8,24,1152]{2,1,0:T(8,128)(2,1)}), bf16[8,24,1152]{2,1,0:T(8,128)(2,1)S(1)}, u32[]{:S(2)}, u32[]{:S(2)}) async-start(bf16[8,24,1152]{2,1,0:T(8,128)(2,1)} %bitcast.15), calls=%async_computation.3 | async-start | bytes 884736 | tf_op jit(solution)/shard_map/all_to_all | solution.py:50
  80.6 1.1 convolution_convert_fusion
  81.8 15.1 %all-to-all-done.3 = bf16[8,24,1152]{2,1,0:T(8,128)(2,1)S(1)} async-done(((bf16[8,24,1152]{2,1,0:T(8,128)(2,1)}), bf16[8,24,1152]{2,1,0:T(8,128)(2,1)S(1)}, u32[]{:S(2)}, u32[]{:S(2)}) %all-to-all-start.3) | async-done | bytes 442400 | tf_op jit(solution)/shard_map/all_to_all | solution.py:50
  96.9 7.5 %all-to-all-start.6 = ((bf16[16,64,256]{2,1,0:T(8,128)(2,1)}), bf16[16,64,256]{2,1,0:T(8,128)(2,1)S(1)}, u32[]{:S(2)}, u32[]{:S(2)}) async-start(bf16[16,64,256]{2,1,0:T(8,128)(2,1)} %bitcast.20), calls=%async_computation.6 | async-start | bytes 1048576 | tf_op jit(solution)/shard_map/all_to_all | solution.py:146
  105.4 9.9 %all-to-all-done.6 = bf16[16,64,256]{2,1,0:T(8,128)(2,1)S(1)} async-done(((bf16[16,64,256]{2,1,0:T(8,128)(2,1)}), bf16[16,64,256]{2,1,0:T(8,128)(2,1)S(1)}, u32[]{:S(2)}, u32[]{:S(2)}) %all-to-all-start.6) | async-done | bytes 524320 | tf_op jit(solution)/shard_map/all_to_all | solution.py:146
  116.2 3.5 %all-to-all-start.4 = ((bf16[8,24,1152]{2,1,0:T(8,128)(2,1)}), bf16[8,24,1152]{2,1,0:T(8,128)(2,1)S(1)}, u32[]{:S(2)}, u32[]{:S(2)}) async-start(bf16[8,24,1152]{2,1,0:T(8,128)(2,1)} %broadcast_in_dim.175), calls=%async_computation.4 | async-start | bytes 884736 | tf_op jit(solution)/shard_map/all_to_all | solution.py:50
  120.3 13.4 %all-to-all-done.4 = bf16[8,24,1152]{2,1,0:T(8,128)(2,1)S(1)} async-done(((bf16[8,24,1152]{2,1,0:T(8,128)(2,1)}), bf16[8,24,1152]{2,1,0:T(8,128)(2,1)S(1)}, u32[]{:S(2)}, u32[]{:S(2)}) %all-to-all-start.4) | async-done | bytes 442400 | tf_op jit(solution)/shard_map/all_to_all | solution.py:50
  134.4 1.2 convolution_bitcast_fusion.2
  135.7 1.2 convolution_bitcast_fusion.1
  138.2 1.2 convolution_convert_fusion.1
  139.4 5.7 %all-to-all-start.5 = ((bf16[16,64,256]{2,1,0:T(8,128)(2,1)}), bf16[16,64,256]{2,1,0:T(8,128)(2,1)S(1)}, u32[]{:S(2)}, u32[]{:S(2)}) async-start(bf16[16,64,256]{2,1,0:T(8,128)(2,1)} %bitcast.19), calls=%async_computation.5 | async-start | bytes 1048576 | tf_op jit(solution)/shard_map/all_to_all | solution.py:146
  146.0 1.0 convolution_convert_fusion.3
  147.0 8.5 %all-to-all-done.5 = bf16[16,64,256]{2,1,0:T(8,128)(2,1)S(1)} async-done(((bf16[16,64,256]{2,1,0:T(8,128)(2,1)}), bf16[16,64,256]{2,1,0:T(8,128)(2,1)S(1)}, u32[]{:S(2)}, u32[]{:S(2)}) %all-to-all-start.5) | async-done | bytes 524320 | tf_op jit(solution)/shard_map/all_to_all | solution.py:146
  (123 shorter events, 19.4 us)
Async XLA Ops:
  3.4 1.5 collective-permute-start.3
  3.5 1.7 %collective-permute-start.4 = (bf16[96,1024]{1,0:T(8,128)(2,1)S(1)}, bf16[96,1024]{1,0:T(8,128)(2,1)S(1)}, u32[]{:S(2)}, u32[]{:S(2)}) collective-permute-start(bf16[96,1024]{1,0:T(8,128)(2,1)S(1)} %get-tuple-element.25), channel_id=1, source_target_pairs={{0,1},{1,0},{2,3},{3,2},{4,5},{5,4},{6,7},{7,6},{8,9},{9,8},{10,11... | collective-permute-start | bytes 589832 | tf_op jit(solution)/shard_map/ppermute | solution.py:46
  6.5 23.6 %all-to-all-start.1 = ((bf16[8,24,1024]{2,1,0:T(8,128)(2,1)}), bf16[8,24,1024]{2,1,0:T(8,128)(2,1)S(1)}, u32[]{:S(2)}, u32[]{:S(2)}) async-start(bf16[8,24,1024]{2,1,0:T(8,128)(2,1)} %bitcast.9), calls=%async_computation.1 | async-start | bytes 786432 | tf_op jit(solution)/shard_map/all_to_all | solution.py:50
  15.3 0.7 collective-permute-start
  30.8 19.6 %all-to-all-start = ((bf16[8,24,1152]{2,1,0:T(8,128)(2,1)}), bf16[8,24,1152]{2,1,0:T(8,128)(2,1)S(1)}, u32[]{:S(2)}, u32[]{:S(2)}) async-start(bf16[8,24,1152]{2,1,0:T(8,128)(2,1)} %broadcast_in_dim.157), calls=%async_computation | async-start | bytes 884736 | tf_op jit(solution)/shard_map/all_to_all | solution.py:50
  34.3 16.0 %collective-permute-start.5 = (bf16[24,1024]{1,0:T(8,128)(2,1)S(1)}, bf16[24,1024]{1,0:T(8,128)(2,1)S(1)}, u32[]{:S(2)}, u32[]{:S(2)}) collective-permute-start(bf16[24,1024]{1,0:T(8,128)(2,1)S(1)} %reduce_sum.67), channel_id=1, source_target_pairs={{0,0},{1,17},{2,34},{3,51},{4,68},{5,85},{6,102},{7,119},{8,136},{... | collective-permute-start | bytes 147464 | tf_op jit(solution)/shard_map/ppermute | solution.py:56
  51.2 19.3 %copy-start.5 = (bf16[1,1024,168]{1,2,0:T(8,128)(2,1)S(1)}, bf16[1,1024,168]{1,2,0:T(8,128)(2,1)}, u32[]{:S(2)}) copy-start(bf16[1,1024,168]{1,2,0:T(8,128)(2,1)} %param.18) | copy-start | bytes 1032196
  51.2 18.7 %all-to-all-start.2 = ((bf16[8,24,1024]{2,1,0:T(8,128)(2,1)}), bf16[8,24,1024]{2,1,0:T(8,128)(2,1)S(1)}, u32[]{:S(2)}, u32[]{:S(2)}) async-start(bf16[8,24,1024]{2,1,0:T(8,128)(2,1)} %broadcast_in_dim.158), calls=%async_computation.2 | async-start | bytes 786432 | tf_op jit(solution)/shard_map/all_to_all | solution.py:50
  54.8 1.6 %collective-permute-start.2 = (bf16[96,1152]{1,0:T(8,128)(2,1)S(1)}, bf16[96,1152]{1,0:T(8,128)(2,1)S(1)}, u32[]{:S(2)}, u32[]{:S(2)}) collective-permute-start(bf16[96,1152]{1,0:T(8,128)(2,1)S(1)} %bitcast.69), channel_id=1, source_target_pairs={{0,1},{1,0},{2,3},{3,2},{4,5},{5,4},{6,7},{7,6},{8,9},{9,8},{10,11... | collective-permute-start | bytes 663560 | tf_op jit(solution)/shard_map/ppermute | solution.py:46
  54.9 1.8 %collective-permute-start.1 = (bf16[96,1152]{1,0:T(8,128)(2,1)S(1)}, bf16[96,1152]{1,0:T(8,128)(2,1)S(1)}, u32[]{:S(2)}, u32[]{:S(2)}) collective-permute-start(bf16[96,1152]{1,0:T(8,128)(2,1)S(1)} %bitcast.68), channel_id=1, source_target_pairs={{0,1},{1,0},{2,3},{3,2},{4,5},{5,4},{6,7},{7,6},{8,9},{9,8},{10,11... | collective-permute-start | bytes 663560 | tf_op jit(solution)/shard_map/ppermute | solution.py:46
  57.4 14.3 %copy-start.19 = (bf16[1,168,1024]{2,1,0:T(8,128)(2,1)S(1)}, bf16[1,168,1024]{2,1,0:T(8,128)(2,1)}, u32[]{:S(2)}) copy-start(bf16[1,168,1024]{2,1,0:T(8,128)(2,1)} %param.19) | copy-start | bytes 1032196
  69.9 1.5 collective-permute-start.7
  70.0 1.7 %collective-permute-start.6 = (bf16[96,1024]{1,0:T(8,128)(2,1)S(1)}, bf16[96,1024]{1,0:T(8,128)(2,1)S(1)}, u32[]{:S(2)}, u32[]{:S(2)}) collective-permute-start(bf16[96,1024]{1,0:T(8,128)(2,1)S(1)} %bitcast.71), channel_id=1, source_target_pairs={{0,1},{1,0},{2,3},{3,2},{4,5},{5,4},{6,7},{7,6},{8,9},{9,8},{10,11... | collective-permute-start | bytes 589832 | tf_op jit(solution)/shard_map/ppermute | solution.py:46
  73.3 1.7 %collective-permute-start.8 = (bf16[96,1152]{0,1:T(8,128)(2,1)S(1)}, bf16[96,1152]{0,1:T(8,128)(2,1)S(1)}, u32[]{:S(2)}, u32[]{:S(2)}) collective-permute-start(bf16[96,1152]{0,1:T(8,128)(2,1)S(1)} %get-tuple-element.14), channel_id=1, source_target_pairs={{0,1},{1,0},{2,3},{3,2},{4,5},{5,4},{6,7},{7,6},{8,9},{9,8},{10,11... | collective-permute-start | bytes 663560 | tf_op jit(solution)/shard_map/ppermute | solution.py:46
  73.6 1.8 %collective-permute-start.9 = (bf16[96,1152]{0,1:T(8,128)(2,1)S(1)}, bf16[96,1152]{0,1:T(8,128)(2,1)S(1)}, u32[]{:S(2)}, u32[]{:S(2)}) collective-permute-start(bf16[96,1152]{0,1:T(8,128)(2,1)S(1)} %get-tuple-element.15), channel_id=1, source_target_pairs={{0,1},{1,0},{2,3},{3,2},{4,5},{5,4},{6,7},{7,6},{8,9},{9,8},{10,11... | collective-permute-start | bytes 663560 | tf_op jit(solution)/shard_map/ppermute | solution.py:46
  77.1 19.8 %all-to-all-start.3 = ((bf16[8,24,1152]{2,1,0:T(8,128)(2,1)}), bf16[8,24,1152]{2,1,0:T(8,128)(2,1)S(1)}, u32[]{:S(2)}, u32[]{:S(2)}) async-start(bf16[8,24,1152]{2,1,0:T(8,128)(2,1)} %bitcast.15), calls=%async_computation.3 | async-start | bytes 884736 | tf_op jit(solution)/shard_map/all_to_all | solution.py:50
  96.9 18.5 %all-to-all-start.6 = ((bf16[16,64,256]{2,1,0:T(8,128)(2,1)}), bf16[16,64,256]{2,1,0:T(8,128)(2,1)S(1)}, u32[]{:S(2)}, u32[]{:S(2)}) async-start(bf16[16,64,256]{2,1,0:T(8,128)(2,1)} %bitcast.20), calls=%async_computation.6 | async-start | bytes 1048576 | tf_op jit(solution)/shard_map/all_to_all | solution.py:146
  104.4 30.0 %copy-start.10 = (bf16[384,168]{0,1:T(8,128)(2,1)S(1)}, bf16[384,168]{0,1:T(8,128)(2,1)}, u32[]{:S(2)}) copy-start(bf16[384,168]{0,1:T(8,128)(2,1)} %copy-done.9) | copy-start | bytes 387076
  104.7 10.6 %collective-permute-start.10 = (bf16[24,1152]{1,0:T(8,128)(2,1)S(1)}, bf16[24,1152]{1,0:T(8,128)(2,1)S(1)}, u32[]{:S(2)}, u32[]{:S(2)}) collective-permute-start(bf16[24,1152]{1,0:T(8,128)(2,1)S(1)} %pad_maximum_fusion.11), channel_id=1, source_target_pairs={{0,0},{1,17},{2,34},{3,51},{4,68},{5,85},{6,102},{7,119},{8,136},{... | collective-permute-start | bytes 165896 | tf_op jit(solution)/shard_map/ppermute | solution.py:56
  116.2 17.6 %all-to-all-start.4 = ((bf16[8,24,1152]{2,1,0:T(8,128)(2,1)}), bf16[8,24,1152]{2,1,0:T(8,128)(2,1)S(1)}, u32[]{:S(2)}, u32[]{:S(2)}) async-start(bf16[8,24,1152]{2,1,0:T(8,128)(2,1)} %broadcast_in_dim.175), calls=%async_computation.4 | async-start | bytes 884736 | tf_op jit(solution)/shard_map/all_to_all | solution.py:50
  120.3 15.3 %copy-start.16 = (f32[384]{0:T(512)S(1)}, f32[384]{0:T(512)}, u32[]{:S(2)}) copy-start(f32[384]{0:T(512)} %get-tuple-element.6) | copy-start | bytes 4612
  133.8 3.0 %collective-permute-start.12 = (bf16[96,1152]{1,0:T(8,128)(2,1)S(1)}, bf16[96,1152]{1,0:T(8,128)(2,1)S(1)}, u32[]{:S(2)}, u32[]{:S(2)}) collective-permute-start(bf16[96,1152]{1,0:T(8,128)(2,1)S(1)} %bitcast.67), channel_id=1, source_target_pairs={{0,1},{1,0},{2,3},{3,2},{4,5},{5,4},{6,7},{7,6},{8,9},{9,8},{10,11... | collective-permute-start | bytes 663560 | tf_op jit(solution)/shard_map/ppermute | solution.py:46
  133.9 2.9 %collective-permute-start.11 = (bf16[96,1152]{1,0:T(8,128)(2,1)S(1)}, bf16[96,1152]{1,0:T(8,128)(2,1)S(1)}, u32[]{:S(2)}, u32[]{:S(2)}) collective-permute-start(bf16[96,1152]{1,0:T(8,128)(2,1)S(1)} %bitcast.66), channel_id=1, source_target_pairs={{0,1},{1,0},{2,3},{3,2},{4,5},{5,4},{6,7},{7,6},{8,9},{9,8},{10,11... | collective-permute-start | bytes 663560 | tf_op jit(solution)/shard_map/ppermute | solution.py:46
  139.4 16.1 %all-to-all-start.5 = ((bf16[16,64,256]{2,1,0:T(8,128)(2,1)}), bf16[16,64,256]{2,1,0:T(8,128)(2,1)S(1)}, u32[]{:S(2)}, u32[]{:S(2)}) async-start(bf16[16,64,256]{2,1,0:T(8,128)(2,1)} %bitcast.19), calls=%async_computation.5 | async-start | bytes 1048576 | tf_op jit(solution)/shard_map/all_to_all | solution.py:146
  (22 other events, 75.8 us)
